TPU v7x, 32 devices: a whole 2x2x4 slice. The times are simulated.
32 devices in a mesh: dp: 16 (over z, x, core), seq: 2 (over y).
Axes of the slice: x: 2, y: 2, z: 4, core: 2. Of those that a mesh axis runs over, the one named last changes fastest.
Arguments:
- frames_in: bfloat16 [16, 1500, 768], P('dp', 'seq'), may hold values from -6 to 6
- ln1_gain: bfloat16 [768], P('dp'), may hold values from 0.25 to 1.75
- ln1_bias: bfloat16 [768], P('dp'), may hold values from -1.75 to 1.75
- w_qkv: bfloat16 [768, 2304], P('dp'), may hold values from -2 to 2
- b_qv: bfloat16 [1536], P('dp'), may hold values from -1.25 to 1.25
- w_o: bfloat16 [768, 768], P('dp'), may hold values from -0.875 to 0.875
- b_o: bfloat16 [768], P('dp'), may hold values from -1.75 to 1.75
- ln2_gain: bfloat16 [768], P('dp'), may hold values from 0.25 to 1.75
- ln2_bias: bfloat16 [768], P('dp'), may hold values from -1.75 to 1.75
- w_fc1: bfloat16 [768, 3072], P('dp'), may hold values from -0.21875 to 0.21875
- b_fc1: bfloat16 [3072], P('dp'), may hold values from -3 to 3
- w_fc2: bfloat16 [3072, 768], P('dp'), may hold values from -0.109375 to 0.109375
- b_fc2: bfloat16 [768], P('dp'), may hold values from -1.75 to 1.75
- cotangent: bfloat16 [16, 1500, 768], P('dp', 'seq'), may hold values from -6 to 6
Outputs:
- frames_out: bfloat16 [16, 1500, 768], P('dp', 'seq')
- grad_frames: float32 [16, 1500, 768], P('dp', 'seq')
- grad_ln1_gain: float32 [768], P('dp')
- grad_ln1_bias: float32 [768], P('dp')
- grad_w_qkv: float32 [768, 2304], P('dp')
- grad_b_qv: float32 [1536], P('dp')
- grad_w_o: float32 [768, 768], P('dp')
- grad_b_o: float32 [768], P('dp')
- grad_ln2_gain: float32 [768], P('dp')
- grad_ln2_bias: float32 [768], P('dp')
- grad_w_fc1: float32 [768, 3072], P('dp')
- grad_b_fc1: float32 [3072], P('dp')
- grad_w_fc2: float32 [3072, 768], P('dp')
- grad_b_fc2: float32 [768], P('dp')
All inputs are finite; a program needn't handle non-finite values.
Results may differ from a plain program's by a relative error of at most 0.0095.
Values may be sent and summed in bfloat16 or wider, within the bound.
No kernel may reach another device: no remote copies, remote signals or barrier semaphores. Data moves between devices by JAX's collectives and lax.ppermute only.
A program may use at most 192 MiB of HBM per device.

v0:
```python
import math
import jax
import jax.numpy as jnp
from jax import lax
from jax.sharding import PartitionSpec as P

HEADS = 12
EPSILON = 1e-05


def normalize(values, gain, shift):
    center = jnp.mean(values, axis=-1, keepdims=True)
    centered = values - center
    variance = jnp.mean(centered * centered, axis=-1, keepdims=True)
    inverse = lax.rsqrt(variance + EPSILON)
    normed = centered * inverse
    return (normed, inverse, normed * gain + shift)


def norm_back(grad_out, normed, inverse, gain):
    weighted = grad_out * gain
    first = jnp.mean(weighted, axis=-1, keepdims=True)
    second = jnp.mean(weighted * normed, axis=-1, keepdims=True)
    return inverse * (weighted - first - normed * second)


def gelu_cdf(values):
    return 0.5 * (1.0 + lax.erf(values * (1.0 / math.sqrt(2.0))))


def gelu_slope(values):
    density = jnp.exp(-0.5 * values * values) * (1.0 / math.sqrt(2.0 * math.pi))
    return gelu_cdf(values) + values * density


def head_forward(operands):
    query, key_rows, value_rows = operands
    factor = 1.0 / math.sqrt(query.shape[-1])
    scores = jnp.dot(query, key_rows.T, preferred_element_type=jnp.float32) * factor
    row_peak = jnp.max(scores, axis=-1, keepdims=True)
    row_total = jnp.sum(jnp.exp(scores - row_peak), axis=-1, keepdims=True)
    logsum = row_peak + jnp.log(row_total)
    weights_low = jnp.exp(scores - logsum).astype(jnp.bfloat16)
    context = jnp.dot(weights_low, value_rows, preferred_element_type=jnp.float32).astype(
        jnp.bfloat16
    )
    return (context, logsum[:, 0])


def head_backward(operands):
    query, key_rows, value_rows, context, grad_context, logsum = operands
    factor = 1.0 / math.sqrt(query.shape[-1])
    scores = jnp.dot(query, key_rows.T, preferred_element_type=jnp.float32) * factor
    weights_full = jnp.exp(scores - logsum[:, None])
    weights_low = weights_full.astype(jnp.bfloat16)
    grad_values = jnp.dot(weights_low.T, grad_context, preferred_element_type=jnp.float32).astype(
        jnp.bfloat16
    )
    grad_weights = jnp.dot(grad_context, value_rows.T, preferred_element_type=jnp.float32)
    delta = jnp.sum(
        grad_context.astype(jnp.float32) * context.astype(jnp.float32), axis=-1, keepdims=True
    )
    grad_scores = (weights_full * (grad_weights - delta)).astype(jnp.bfloat16)
    grad_query = (
        jnp.dot(grad_scores, key_rows, preferred_element_type=jnp.float32) * factor
    ).astype(jnp.bfloat16)
    grad_keys = (jnp.dot(grad_scores.T, query, preferred_element_type=jnp.float32) * factor).astype(
        jnp.bfloat16
    )
    return (grad_query, grad_keys, grad_values)


def to_heads(block, head_size):
    clip_count, frame_count, group_width = block.shape
    split = block.reshape(clip_count, frame_count, group_width // head_size, head_size)
    return split.transpose(0, 2, 1, 3).reshape(
        clip_count * (group_width // head_size), frame_count, head_size
    )


def from_heads(block, clip_count):
    stacked, frame_count, head_size = block.shape
    group_heads = stacked // clip_count
    joined = block.reshape(clip_count, group_heads, frame_count, head_size).transpose(0, 2, 1, 3)
    return joined.reshape(clip_count, frame_count, group_heads * head_size)


def shards(
    frames_in,
    ln1_gain,
    ln1_bias,
    w_qkv,
    b_qv,
    w_o,
    b_o,
    ln2_gain,
    ln2_bias,
    w_fc1,
    b_fc1,
    w_fc2,
    b_fc2,
    cotangent,
):
    clip_count, local_frames, features = frames_in.shape
    head_size = features // HEADS
    token_rows = clip_count * local_frames
    shape_local = (clip_count, local_frames, features)
    attn_full = (
        lax.all_gather(w_qkv, "dp", axis=0, tiled=True),
        lax.all_gather(w_o, "dp", axis=0, tiled=True),
        lax.all_gather(ln1_gain, "dp", axis=0, tiled=True),
        lax.all_gather(ln1_bias, "dp", axis=0, tiled=True),
        lax.all_gather(b_qv, "dp", axis=0, tiled=True),
        lax.all_gather(b_o, "dp", axis=0, tiled=True),
    )
    qkv_full, out_full, gain_low_one, shift_low_one, bias_qv_low, bias_out_low = attn_full
    gain_one = gain_low_one.astype(jnp.float32)
    shift_one = shift_low_one.astype(jnp.float32)
    bias_wide = bias_qv_low.astype(jnp.float32)
    bias_out = bias_out_low.astype(jnp.float32)
    inputs = frames_in.reshape(token_rows, features).astype(jnp.float32)
    normed_one, inverse_one, hidden_one = normalize(inputs, gain_one, shift_one)
    hidden_one = hidden_one.astype(jnp.bfloat16)
    projected = jnp.dot(hidden_one, qkv_full, preferred_element_type=jnp.float32)
    query = (projected[:, :features] + bias_wide[:features]).astype(jnp.bfloat16)
    key_rows = projected[:, features : 2 * features].astype(jnp.bfloat16)
    value_rows = (projected[:, 2 * features :] + bias_wide[features:]).astype(jnp.bfloat16)
    query_group, key_group, value_group = (
        lax.all_to_all(query.reshape(shape_local), "seq", split_axis=2, concat_axis=1, tiled=True),
        lax.all_to_all(
            key_rows.reshape(shape_local), "seq", split_axis=2, concat_axis=1, tiled=True
        ),
        lax.all_to_all(
            value_rows.reshape(shape_local), "seq", split_axis=2, concat_axis=1, tiled=True
        ),
    )
    query_heads = to_heads(query_group, head_size)
    key_heads = to_heads(key_group, head_size)
    value_heads = to_heads(value_group, head_size)
    context_heads, logsum = lax.map(head_forward, (query_heads, key_heads, value_heads))
    context_heads = lax.optimization_barrier(context_heads)
    context = lax.all_to_all(
        from_heads(context_heads, clip_count), "seq", split_axis=1, concat_axis=2, tiled=True
    )
    context = context.reshape(token_rows, features)
    residual = inputs + jnp.dot(context, out_full, preferred_element_type=jnp.float32) + bias_out
    mlp_full = (
        lax.all_gather(w_fc1, "dp", axis=0, tiled=True),
        lax.all_gather(w_fc2, "dp", axis=0, tiled=True),
        lax.all_gather(ln2_gain, "dp", axis=0, tiled=True),
        lax.all_gather(ln2_bias, "dp", axis=0, tiled=True),
        lax.all_gather(b_fc1, "dp", axis=0, tiled=True),
        lax.all_gather(b_fc2, "dp", axis=0, tiled=True),
    )
    fc1_full, fc2_full, gain_low_two, shift_low_two, bias_fc1_low, bias_fc2_low = mlp_full
    gain_two = gain_low_two.astype(jnp.float32)
    shift_two = shift_low_two.astype(jnp.float32)
    normed_two, inverse_two, hidden_two = normalize(residual, gain_two, shift_two)
    hidden_two = hidden_two.astype(jnp.bfloat16)
    pre_act = jnp.dot(
        hidden_two, fc1_full, preferred_element_type=jnp.float32
    ) + bias_fc1_low.astype(jnp.float32)
    activated = (pre_act * gelu_cdf(pre_act)).astype(jnp.bfloat16)
    output = (
        residual
        + jnp.dot(activated, fc2_full, preferred_element_type=jnp.float32)
        + bias_fc2_low.astype(jnp.float32)
    )
    frames_out = output.astype(jnp.bfloat16).reshape(shape_local)
    grad_low = cotangent.reshape(token_rows, features)
    grad_full = grad_low.astype(jnp.float32)
    grad_bias_fc2 = jnp.sum(grad_full, axis=0)
    grad_weight_fc2 = jnp.dot(activated.T, grad_low, preferred_element_type=jnp.float32)
    grad_pre = jnp.dot(grad_low, fc2_full.T, preferred_element_type=jnp.float32) * gelu_slope(
        pre_act
    )
    grad_bias_fc1 = jnp.sum(grad_pre, axis=0)
    grad_pre_low = grad_pre.astype(jnp.bfloat16)
    grad_weight_fc1 = jnp.dot(hidden_two.T, grad_pre_low, preferred_element_type=jnp.float32)
    grad_hidden_two = jnp.dot(grad_pre_low, fc1_full.T, preferred_element_type=jnp.float32)
    grad_gain_two = jnp.sum(grad_hidden_two * normed_two, axis=0)
    grad_shift_two = jnp.sum(grad_hidden_two, axis=0)
    grad_residual = grad_full + norm_back(grad_hidden_two, normed_two, inverse_two, gain_two)
    mlp_terms = (
        grad_weight_fc1,
        grad_weight_fc2,
        grad_gain_two,
        grad_shift_two,
        grad_bias_fc1,
        grad_bias_fc2,
    )
    mlp_summed = lax.psum(
        (mlp_terms[0], mlp_terms[1], mlp_terms[2], mlp_terms[3], mlp_terms[4], mlp_terms[5]), "seq"
    )
    mlp_grads = (
        lax.psum_scatter(mlp_summed[0], "dp", scatter_dimension=0, tiled=True),
        lax.psum_scatter(mlp_summed[1], "dp", scatter_dimension=0, tiled=True),
        lax.psum_scatter(mlp_summed[2], "dp", scatter_dimension=0, tiled=True),
        lax.psum_scatter(mlp_summed[3], "dp", scatter_dimension=0, tiled=True),
        lax.psum_scatter(mlp_summed[4], "dp", scatter_dimension=0, tiled=True),
        lax.psum_scatter(mlp_summed[5], "dp", scatter_dimension=0, tiled=True),
    )
    grad_bias_out = jnp.sum(grad_residual, axis=0)
    grad_residual_low = grad_residual.astype(jnp.bfloat16)
    grad_weight_out = jnp.dot(context.T, grad_residual_low, preferred_element_type=jnp.float32)
    grad_context = jnp.dot(
        grad_residual_low, out_full.T, preferred_element_type=jnp.float32
    ).astype(jnp.bfloat16)
    grad_context_group = lax.all_to_all(
        grad_context.reshape(shape_local), "seq", split_axis=2, concat_axis=1, tiled=True
    )
    back_heads = lax.map(
        head_backward,
        (
            query_heads,
            key_heads,
            value_heads,
            context_heads,
            to_heads(grad_context_group, head_size),
            logsum,
        ),
    )
    grad_query_back, grad_keys_back, grad_values_back = (
        lax.all_to_all(
            from_heads(back_heads[0], clip_count), "seq", split_axis=1, concat_axis=2, tiled=True
        ),
        lax.all_to_all(
            from_heads(back_heads[1], clip_count), "seq", split_axis=1, concat_axis=2, tiled=True
        ),
        lax.all_to_all(
            from_heads(back_heads[2], clip_count), "seq", split_axis=1, concat_axis=2, tiled=True
        ),
    )
    grad_query = grad_query_back.reshape(token_rows, features)
    grad_keys = grad_keys_back.reshape(token_rows, features)
    grad_values = grad_values_back.reshape(token_rows, features)
    grad_bias_qv = jnp.concatenate(
        [
            jnp.sum(grad_query.astype(jnp.float32), axis=0),
            jnp.sum(grad_values.astype(jnp.float32), axis=0),
        ]
    )
    grad_projected = jnp.concatenate([grad_query, grad_keys, grad_values], axis=1)
    grad_weight_qkv = jnp.dot(hidden_one.T, grad_projected, preferred_element_type=jnp.float32)
    grad_hidden_one = jnp.dot(grad_projected, qkv_full.T, preferred_element_type=jnp.float32)
    grad_gain_one = jnp.sum(grad_hidden_one * normed_one, axis=0)
    grad_shift_one = jnp.sum(grad_hidden_one, axis=0)
    grad_input = grad_residual + norm_back(grad_hidden_one, normed_one, inverse_one, gain_one)
    attn_terms = (
        grad_weight_qkv,
        grad_weight_out,
        grad_gain_one,
        grad_shift_one,
        grad_bias_qv,
        grad_bias_out,
    )
    attn_summed = lax.psum(
        (attn_terms[0], attn_terms[1], attn_terms[2], attn_terms[3], attn_terms[4], attn_terms[5]),
        "seq",
    )
    attn_grads = (
        lax.psum_scatter(attn_summed[0], "dp", scatter_dimension=0, tiled=True),
        lax.psum_scatter(attn_summed[1], "dp", scatter_dimension=0, tiled=True),
        lax.psum_scatter(attn_summed[2], "dp", scatter_dimension=0, tiled=True),
        lax.psum_scatter(attn_summed[3], "dp", scatter_dimension=0, tiled=True),
        lax.psum_scatter(attn_summed[4], "dp", scatter_dimension=0, tiled=True),
        lax.psum_scatter(attn_summed[5], "dp", scatter_dimension=0, tiled=True),
    )
    return (
        frames_out,
        grad_input.reshape(shape_local),
        attn_grads[2],
        attn_grads[3],
        attn_grads[0],
        attn_grads[4],
        attn_grads[1],
        attn_grads[5],
        mlp_grads[2],
        mlp_grads[3],
        mlp_grads[0],
        mlp_grads[4],
        mlp_grads[1],
        mlp_grads[5],
    )


def solution(mesh):
    in_specs = (
        P("dp", "seq", None),
        P("dp"),
        P("dp"),
        P("dp", None),
        P("dp"),
        P("dp", None),
        P("dp"),
        P("dp"),
        P("dp"),
        P("dp", None),
        P("dp"),
        P("dp", None),
        P("dp"),
        P("dp", "seq", None),
    )
    out_specs = (
        P("dp", "seq", None),
        P("dp", "seq", None),
        P("dp"),
        P("dp"),
        P("dp", None),
        P("dp"),
        P("dp", None),
        P("dp"),
        P("dp"),
        P("dp"),
        P("dp", None),
        P("dp"),
        P("dp", None),
        P("dp"),
    )
    return jax.shard_map(shards, mesh=mesh, in_specs=in_specs, out_specs=out_specs, check_vma=False)
```

profile of v0, /device:TPU:0, one launch (start us, length us, event | category | flops | bytes accessed | tf_op | source)
XLA Modules:
  0.0 1038.6 jit_solution(15430332601258797024)
XLA Ops:
  19.4 64.0 %all-reduce.19 = (bf16[1536]{0:T(1024)(128)(2,1)S(1)}, bf16[768]{0:T(1024)(128)(2,1)S(1)}, bf16[768]{0:T(1024)(128)(2,1)S(1)}, bf16[768]{0:T(1024)(128)(2,1)S(1)...) all-reduce(bf16[1536]{0:T(1024)(128)(2,1)S(1)} %dynamic-update-slic, ...), channel_id=1, replica_groups=mesh['dp'=16,'seq'=2] {'dp'}, use_global_device_ids=true, to_apply=%add.2 | all-reduce | flops 9216 | bytes 36864
  85.5 5.1 fusion.88
  93.8 4.7 copy.76
  99.0 9.1 reduce.13
  108.1 4.6 reshape.282
  112.7 4.6 all-to-all-start
  117.3 4.7 copy.80
  122.0 9.1 reduce.15
  131.1 4.1 reshape.286
  135.2 4.5 all-to-all-start.2
  141.5 4.8 copy.78
  146.3 9.1 reduce.14
  155.4 4.1 reshape.284
  159.6 4.5 all-to-all-start.1
  164.6 5.4 reshape.283
  177.6 5.2 reshape.287
  186.9 4.0 reshape.208
  194.6 5.2 reshape.285
  203.9 4.4 reshape.205
  213.2 42.6 %while.26 = (s32[]{:T(128)}, bf16[6,1500,64]{1,2,0:T(8,128)(2,1)}, f32[6,1500]{1,0:T(8,128)S(1)}, bf16[6,1500,64]{2,1,0:T(8,128)(2,1)S(1)}, bf16[6,1500,64]{2,1,...) while((s32[]{:T(128)}, bf16[6,1500,64]{1,2,0:T(8,128)(2,1)}, ...), condition=%wide.region_5.6_spmd, body=%wide.region_2.5_spmd.sunk | while | flops 589594496 | bytes 28419816 | solution.py:140
  255.8 6.6 copy.85
  262.4 10.9 %reduce.16 = bf16[1500,384]{1,0:T(8,128)(2,1)} reduce(bf16[1500,1,384]{2,1,0:T(2,128)(2,1)} %bitcast.268, bf16[]{:T(256)} %broadcast.144), dimensions={1}, to_apply=%bitcast.180.reduce_sub_computation | reduce | bytes 2304002
  273.3 3.8 reshape.288
  277.1 4.4 all-to-all-start.3
  281.6 10.9 %all-to-all-done.3 = bf16[2,2,144000]{2,1,0:T(2,128)(2,1)} async-done(((bf16[2,2,144000]{2,1,0:T(2,128)(2,1)}), bf16[2,2,144000]{2,1,0:T(2,128)(2,1)}, u32[]{:S(2)}, u32[]{:S(2)}) %all-to-all-start.3) | async-done | bytes 1152032 | tf_op jit(solution)/shard_map/all_to_all | solution.py:142
  292.5 5.7 reshape.289
  298.1 10.9 %bitcast_reduce_fusion.3 = bf16[1500,384]{1,0:T(8,128)(2,1)} fusion(bf16[1500,1,384]{2,1,0:T(2,128)(2,1)} %reshape.289), kind=kLoop, calls=%fused_computation.142 | loop fusion | bytes 2304000 | tf_op jit(solution)/shard_map/all_to_all | solution.py:142
  318.6 10.8 %multiply_convert_fusion = (bf16[750,3072]{1,0:T(8,128)(2,1)}, f32[750,3072]{1,0:T(8,128)}) fusion(f32[3072]{0:T(1024)S(1)} %convert_element_type.111, bf16[768,3072]{1,0:T(8,128)(2,1)} %all-gather.9.cloned.1.call-done, f32[750,768]{1,0:T(8,128)} %copy-done, f32[768]{0:T(1024)S(1)} %convert_element_type.109, f32[768]{0:T(1024)S(1)} %convert_element_type.108, ...), kind=kOutput, calls=%fused_computation.62 | convolution fusion | flops 3555648000 | bytes 20871024 | tf_op jit(solution)/shard_map/dot_general | solution.py:160
  329.5 10.2 fusion.96
  339.7 4.8 multiply_reduce_fusion
  348.8 4.7 copy.87
  353.5 9.1 reduce.17
  362.6 4.6 reshape.290
  370.9 4.5 fusion.82
  375.4 5.4 all-to-all-done.4
  380.7 4.1 reshape.291
  393.2 93.8 %while.27 = (s32[]{:T(128)}, bf16[6,1500,64]{1,2,0:T(8,128)(2,1)}, bf16[6,1500,64]{1,2,0:T(8,128)(2,1)}, bf16[6,1500,64]{1,2,0:T(8,128)(2,1)}, bf16[6,1500,64]{2...) while((s32[]{:T(128)}, bf16[6,1500,64]{1,2,0:T(8,128)(2,1)}, ...), condition=%wide.region_12.13_spmd, body=%wide.region_10.12_spmd.sunk | while | flops 1454362368 | bytes 45485876 | solution.py:212
  487.0 6.8 copy.94
  493.8 10.0 reduce.20
  503.8 3.9 reshape.296
  507.7 4.4 all-to-all-start.5
  512.1 4.1 copy.96
  516.3 9.9 reduce.19
  526.1 3.9 reshape.294
  530.0 4.5 all-to-all-start.6
  534.5 4.1 copy.98
  538.7 8.8 reduce.18
  550.1 4.5 reshape.297
  554.6 4.5 all-to-all-start.7
  559.1 10.1 bitcast_reduce_fusion
  572.1 4.5 reshape.295
  576.6 9.9 bitcast_reduce_fusion.1
  589.5 4.5 reshape.293
  594.0 9.9 bitcast_reduce_fusion.2
  607.3 8.3 fusion.72
  617.3 8.9 fusion.68
  626.3 10.9 %fusion.79 = f32[3072,768]{1,0:T(8,128)} fusion(bf16[750,3072]{1,0:T(8,128)(2,1)} %get-tuple-element.303, bf16[1,750,768]{2,1,0:T(8,128)(2,1)} %param.31), kind=kOutput, calls=%fused_computation.114 | convolution fusion | flops 3538944000 | bytes 15197184 | tf_op jit(solution)/shard_map/dot_general | solution.py:173
  639.4 9.1 fusion.75
  650.3 60.8 %reduce-scatter.5.cloned.1.call-done = f32[48,2304]{1,0:T(8,128)} async-done(((f32[768,2304]{1,0:T(8,128)}), f32[48,2304]{1,0:T(8,128)}) %reduce-scatter.5.cloned.1.call-update) | async-done | bytes 442384 | tf_op jit(solution)/shard_map/reduce_scatter | solution.py:262
  711.1 115.0 %reduce-scatter.9.cloned.1.call-done = f32[48,3072]{1,0:T(8,128)} async-done(((f32[768,3072]{1,0:T(8,128)}), f32[48,3072]{1,0:T(8,128)}) %reduce-scatter.9.cloned.1.call-update) | async-done | bytes 589840 | tf_op jit(solution)/shard_map/reduce_scatter | solution.py:196
  826.2 115.0 %reduce-scatter.11.cloned.1.call-done = f32[192,768]{1,0:T(8,128)} async-done(((f32[3072,768]{1,0:T(8,128)}), f32[192,768]{1,0:T(8,128)}) %reduce-scatter.11.cloned.1.call-update) | async-done | bytes 589840 | tf_op jit(solution)/shard_map/reduce_scatter | solution.py:197
  941.3 7.9 fusion.63
  949.3 60.9 %all-reduce.16 = (f32[768]{0:T(1024)S(1)}, f32[768]{0:T(1024)}, f32[1536]{0:T(1024)S(1)}, f32[768]{0:T(1024)}, f32[768]{0:T(1024)}, /*index=5*/f32[768]{0:T(1024)}, f32[3072]{0:T(1024)S(1)}, f32[768]{0:T(1024)}) all-reduce(f32[768]{0:T(1024)S(1)} %get-tuple-element.222, ...), channel_id=2, replica_groups=mesh['dp'=16,'seq'=2] {'dp'}, use_global_device_ids=true, to_apply=%region_17.18.clone | all-reduce | flops 9216 | bytes 73728
  1020.1 5.5 all-reduce.17
  (278 shorter events, 236.5 us)
Async XLA Ops:
  7.2 77.7 %copy-start.4 = (bf16[1,750,768]{2,1,0:T(8,128)(2,1)S(1)}, bf16[1,750,768]{2,1,0:T(8,128)(2,1)}, u32[]{:S(2)}) copy-start(bf16[1,750,768]{2,1,0:T(8,128)(2,1)} %param.18) | copy-start | bytes 3456004
  7.2 78.3 %all-gather.5.cloned.1.call-start = ((), (), s32[]{:S(2)}) async-start(), calls=%async_computation.12 | async-start | bytes 3760128 | tf_op jit(solution)/shard_map/all_gather | solution.py:109
  7.9 306.0 %all-gather.7.cloned.1.call-start = ((), (), s32[]{:S(2)}) async-start(), calls=%async_computation.13 | async-start | bytes 1253376 | tf_op jit(solution)/shard_map/all_gather | solution.py:110
  8.7 309.9 %all-gather.9.cloned.1.call-start = ((), (), s32[]{:S(2)}) async-start(), calls=%async_computation.14 | async-start | bytes 5013504 | tf_op jit(solution)/shard_map/all_gather | solution.py:148
  83.4 7.2 copy-start.20
  83.4 7.2 copy-start.25
  84.9 5.7 copy-start.16
  85.4 5.2 copy-start.22
  90.6 3.2 copy-start.9
  112.7 4.6 copy-start.13
  112.7 22.6 %all-to-all-start = ((bf16[2,2,144000]{2,1,0:T(2,128)(2,1)}), bf16[2,2,144000]{2,1,0:T(2,128)(2,1)}, u32[]{:S(2)}, u32[]{:S(2)}) async-start(bf16[2,2,144000]{2,1,0:T(2,128)(2,1)} %reshape.282), calls=%async_computation | async-start | bytes 2304000 | tf_op jit(solution)/shard_map/all_to_all | solution.py:129
  135.2 24.3 %all-to-all-start.2 = ((bf16[2,2,144000]{2,1,0:T(2,128)(2,1)}), bf16[2,2,144000]{2,1,0:T(2,128)(2,1)}, u32[]{:S(2)}, u32[]{:S(2)}) async-start(bf16[2,2,144000]{2,1,0:T(2,128)(2,1)} %reshape.286), calls=%async_computation.2 | async-start | bytes 2304000 | tf_op jit(solution)/shard_map/all_to_all | solution.py:133
  159.6 35.1 %all-to-all-start.1 = ((bf16[2,2,144000]{2,1,0:T(2,128)(2,1)}), bf16[2,2,144000]{2,1,0:T(2,128)(2,1)}, u32[]{:S(2)}, u32[]{:S(2)}) async-start(bf16[2,2,144000]{2,1,0:T(2,128)(2,1)} %reshape.284), calls=%async_computation.1 | async-start | bytes 2304000 | tf_op jit(solution)/shard_map/all_to_all | solution.py:130
  164.0 165.4 %all-gather.11.cloned.1.call-start = ((), (), s32[]{:S(2)}) async-start(), calls=%async_computation.15 | async-start | bytes 5013504 | tf_op jit(solution)/shard_map/all_gather | solution.py:149
  277.1 15.4 %all-to-all-start.3 = ((bf16[2,2,144000]{2,1,0:T(2,128)(2,1)}), bf16[2,2,144000]{2,1,0:T(2,128)(2,1)}, u32[]{:S(2)}, u32[]{:S(2)}) async-start(bf16[2,2,144000]{2,1,0:T(2,128)(2,1)} %reshape.288), calls=%async_computation.3 | async-start | bytes 2304000 | tf_op jit(solution)/shard_map/all_to_all | solution.py:142
  316.8 1.4 copy-start
  318.6 10.9 %copy-start.14 = (bf16[1,750,768]{2,1,0:T(8,128)(2,1)S(1)}, bf16[1,750,768]{2,1,0:T(8,128)(2,1)}, u32[]{:S(2)}) copy-start(bf16[1,750,768]{2,1,0:T(8,128)(2,1)} %param.31) | copy-start | bytes 3456004
  329.5 10.2 copy-start.1
  329.5 10.2 copy-start.30
  339.7 4.8 copy-start.12
  344.5 3.2 copy-start.31
  346.3 1.4 copy-start.7
  367.2 13.5 %all-to-all-start.4 = ((bf16[2,2,144000]{2,1,0:T(2,128)(2,1)}), bf16[2,2,144000]{2,1,0:T(2,128)(2,1)S(1)}, u32[]{:S(2)}, u32[]{:S(2)}) async-start(bf16[2,2,144000]{2,1,0:T(2,128)(2,1)} %reshape.290), calls=%async_computation.4 | async-start | bytes 2304000 | tf_op jit(solution)/shard_map/all_to_all | solution.py:209
  370.8 279.5 %reduce-scatter.7.cloned.1.call-start = ((), (), s32[]{:S(2)}) async-start(), calls=%async_computation.17 | async-start | bytes 2506752 | tf_op jit(solution)/shard_map/reduce_scatter | solution.py:263
  503.8 8.3 copy-start.10
  507.7 22.4 %all-to-all-start.5 = ((bf16[2,2,144000]{2,1,0:T(2,128)(2,1)}), bf16[2,2,144000]{2,1,0:T(2,128)(2,1)}, u32[]{:S(2)}, u32[]{:S(2)}) async-start(bf16[2,2,144000]{2,1,0:T(2,128)(2,1)} %reshape.296), calls=%async_computation.5 | async-start | bytes 2304000 | tf_op jit(solution)/shard_map/all_to_all | solution.py:224
  526.1 8.4 copy-start.11
  530.0 24.5 %all-to-all-start.6 = ((bf16[2,2,144000]{2,1,0:T(2,128)(2,1)}), bf16[2,2,144000]{2,1,0:T(2,128)(2,1)}, u32[]{:S(2)}, u32[]{:S(2)}) async-start(bf16[2,2,144000]{2,1,0:T(2,128)(2,1)} %reshape.294), calls=%async_computation.6 | async-start | bytes 2304000 | tf_op jit(solution)/shard_map/all_to_all | solution.py:227
  554.6 34.9 %all-to-all-start.7 = ((bf16[2,2,144000]{2,1,0:T(2,128)(2,1)}), bf16[2,2,144000]{2,1,0:T(2,128)(2,1)}, u32[]{:S(2)}, u32[]{:S(2)}) async-start(bf16[2,2,144000]{2,1,0:T(2,128)(2,1)} %reshape.292), calls=%async_computation.7 | async-start | bytes 2304000 | tf_op jit(solution)/shard_map/all_to_all | solution.py:230
  559.1 152.1 %reduce-scatter.5.cloned.1.call-start = ((), (), s32[]{:S(2)}) async-start(), calls=%async_computation.16 | async-start | bytes 7520256 | tf_op jit(solution)/shard_map/reduce_scatter | solution.py:262
  603.8 3.5 copy-start.5
  603.8 3.5 copy-start.17
  603.8 3.5 copy-start.21
  603.8 3.5 copy-start.23
  603.9 3.5 copy-start.26
  605.4 10.2 copy-start.3
  615.6 1.7 copy-start.2
  615.7 210.5 %reduce-scatter.9.cloned.1.call-start = ((), (), s32[]{:S(2)}) async-start(), calls=%async_computation.18 | async-start | bytes 10027008 | tf_op jit(solution)/shard_map/reduce_scatter | solution.py:196
  626.2 315.0 %reduce-scatter.11.cloned.1.call-start = ((), (), s32[]{:S(2)}) async-start(), calls=%async_computation.19 | async-start | bytes 10027008 | tf_op jit(solution)/shard_map/reduce_scatter | solution.py:197
  637.1 2.2 copy-start.29
  637.2 388.5 %all-reduce.22.cloned.1.call-start = ((), (), s32[]{:S(2)}) async-start(), calls=%async_computation.20 | async-start | bytes 3538944 | tf_op jit(solution)/shard_map/psum | solution.py:257
  648.5 292.8 %copy-start.6 = (bf16[1,750,768]{2,1,0:T(8,128)(2,1)S(1)}, bf16[1,750,768]{2,1,0:T(8,128)(2,1)}, u32[]{:S(2)}) copy-start(bf16[1,750,768]{2,1,0:T(8,128)(2,1)} %param.18) | copy-start | bytes 3456004
  941.2 8.0 copy-start.18
  941.2 8.0 copy-start.19
  941.2 8.0 copy-start.24
  941.3 8.0 copy-start.27
  941.3 8.0 copy-start.28
  941.3 72.7 %copy-start.8 = (f32[750,768]{1,0:T(8,128)S(1)}, f32[750,768]{1,0:T(8,128)}, u32[]{:S(2)}) copy-start(f32[750,768]{1,0:T(8,128)} %copy-done.7) | copy-start | bytes 6912004
  1025.7 5.4 copy-start.15
Sparse Core Ops, SparseCore 0:
  10.3 50.1 all-gather.4
  62.8 36.8 all-gather.6
  101.9 51.9 all-gather.8
  166.8 50.9 all-gather.10
  375.5 62.9 reduce-scatter.6
  615.8 95.3 reduce-scatter.4
  715.2 110.9 reduce-scatter.8
  830.3 110.8 reduce-scatter.10
  943.7 55.5 all-reduce.21
where the time goes:
time: 1050 us; the launch traced here: 1040 us
  waiting for transfers between devices  310 us (30%)
  local copies, waits for them, and re-layouts  248 us (24%)
  matrix products  200 us (19%)
  blocking collectives  130 us (12%)
  other arithmetic  95.8 us (9%)
  starting transfers between devices  35.5 us (3%)
  between operations  18.6 us (2%)
    unnamed x2, blocking collectives  125 us
    reduce_scatter x1, waiting for transfers between devices, shards(): lax.psum_scatter(mlp_summed[0], 'dp', scatter_dimension=0, tiled=True)  115 us
    reduce_scatter x1, waiting for transfers between devices, shards(): lax.psum_scatter(mlp_summed[1], 'dp', scatter_dimension=0, tiled=True)  115 us
    unnamed x115, local copies, waits for them, and re-layouts  107 us
    unnamed x8, other arithmetic  76.1 us
    reduce_scatter x1, waiting for transfers between devices, shards(): lax.psum_scatter(attn_summed[0], 'dp', scatter_dimension=0, tiled=True)  60.8 us
    reshape x4, local copies, waits for them, and re-layouts, from_heads(): return joined.reshape(clip_count, frame_count, group_heads * head_size)  21.6 us
  transfers between devices with their start and end apart: 17, of which 5 were waited for; matrix products, arithmetic and copies ran while one was open for 47% of the time, Pallas kernels for 0%

commit v1 on v0

--- a/solution.py
+++ b/solution.py
@@ -139,8 +139,16 @@
     value_heads = to_heads(value_group, head_size)
     context_heads, logsum = lax.map(head_forward, (query_heads, key_heads, value_heads))
     context_heads = lax.optimization_barrier(context_heads)
-    context = lax.all_to_all(
-        from_heads(context_heads, clip_count), "seq", split_axis=1, concat_axis=2, tiled=True
+    context = jnp.concatenate(
+        lax.all_to_all(
+            jnp.stack(
+                jnp.split(from_heads(context_heads, clip_count), lax.axis_size("seq"), axis=1)
+            ),
+            "seq",
+            0,
+            0,
+        ),
+        axis=2,
     )
     context = context.reshape(token_rows, features)
     residual = inputs + jnp.dot(context, out_full, preferred_element_type=jnp.float32) + bias_out

time: 1050 us -> 1020 us (0.971)
  local copies, waits for them, and re-layouts: 248 us -> 222 us
    all_to_all x3 -> x0, local copies, waits for them, and re-layouts: 15.8 us -> none  [shards(): lax.all_to_all(from_heads(context_heads, clip_count), 'seq', split_axis=1...]
    unnamed x8 -> x7, other arithmetic: 76.1 us -> 65.5 us
    unnamed x115 -> x113, local copies, waits for them, and re-layouts: 107 us -> 96.6 us
    reshape x4 -> x3, local copies, waits for them, and re-layouts: 21.6 us -> 15.1 us  [from_heads(): return joined.reshape(clip_count, frame_count, group_heads * head_size)]
  transfers between devices with their start and end apart: 17 -> 17, of which waited for: 5 -> 5; matrix products, arithmetic and copies ran while one was open for 47% -> 45% of each run, Pallas kernels for 0% -> 0%
where the time goes in v1:
time: 1020 us; the launch traced here: 1000 us
  waiting for transfers between devices  310 us (30%)
  local copies, waits for them, and re-layouts  222 us (22%)
  matrix products  200 us (20%)
  blocking collectives  130 us (13%)
  other arithmetic  86.3 us (8%)
  starting transfers between devices  35.6 us (3%)
  between operations  18.8 us (2%)
    unnamed x2, blocking collectives  125 us
    reduce_scatter x1, waiting for transfers between devices, shards(): lax.psum_scatter(mlp_summed[0], 'dp', scatter_dimension=0, tiled=True)  115 us
    reduce_scatter x1, waiting for transfers between devices, shards(): lax.psum_scatter(mlp_summed[1], 'dp', scatter_dimension=0, tiled=True)  115 us
    unnamed x113, local copies, waits for them, and re-layouts  96.6 us
    unnamed x7, other arithmetic  65.5 us
    reduce_scatter x1, waiting for transfers between devices, shards(): lax.psum_scatter(attn_summed[0], 'dp', scatter_dimension=0, tiled=True)  60.9 us
    dot_general x6, matrix products, head_backward(): jnp.dot(grad_context, value_rows.T, preferred_element_type=jnp.float32)  20.6 us
  transfers between devices with their start and end apart: 17, of which 5 were waited for; matrix products, arithmetic and copies ran while one was open for 45% of the time, Pallas kernels for 0%

profile of v1, /device:TPU:0, one launch (start us, length us, event | category | flops | bytes accessed | tf_op | source)
XLA Modules:
  0.0 1003.5 jit_solution(13989843017462850084)
XLA Ops:
  19.4 64.0 %all-reduce.19 = (bf16[1536]{0:T(1024)(128)(2,1)S(1)}, bf16[768]{0:T(1024)(128)(2,1)S(1)}, bf16[768]{0:T(1024)(128)(2,1)S(1)}, bf16[768]{0:T(1024)(128)(2,1)S(1)...) all-reduce(bf16[1536]{0:T(1024)(128)(2,1)S(1)} %dynamic-update-slic, ...), channel_id=1, replica_groups=mesh['dp'=16,'seq'=2] {'dp'}, use_global_device_ids=true, to_apply=%add.2 | all-reduce | flops 9216 | bytes 36864
  85.5 5.1 fusion.88
  93.8 4.7 copy.73
  99.0 9.1 reduce.11
  108.1 4.3 reshape.280
  112.4 4.6 all-to-all-start
  117.0 4.7 copy.77
  121.7 9.1 reduce.13
  130.8 4.1 reshape.284
  135.0 4.5 all-to-all-start.2
  141.2 5.1 copy.75
  146.3 9.1 reduce.12
  155.4 4.1 reshape.282
  159.5 4.5 all-to-all-start.1
  164.6 5.4 reshape.281
  177.6 5.2 reshape.285
  186.9 4.0 reshape.207
  190.9 3.7 copy.81
  194.5 5.2 reshape.283
  203.8 4.2 reshape.204
  208.0 3.8 copy.80
  212.9 42.7 %while.26 = (s32[]{:T(128)}, bf16[6,1500,64]{1,2,0:T(8,128)(2,1)}, f32[6,1500]{1,0:T(8,128)S(1)}, bf16[6,1500,64]{2,1,0:T(8,128)(2,1)S(1)}, bf16[6,1500,64]{2,1,...) while((s32[]{:T(128)}, bf16[6,1500,64]{1,2,0:T(8,128)(2,1)}, ...), condition=%wide.region_5.6_spmd, body=%wide.region_2.5_spmd.sunk | while | flops 589594496 | bytes 28419816 | solution.py:140
  260.6 4.4 all-to-all-start.3
  265.1 11.0 %all-to-all-done.3 = bf16[2,1,750,384]{3,2,1,0:T(8,128)(2,1)} async-done(((bf16[2,1,750,384]{3,2,1,0:T(8,128)(2,1)}), bf16[2,1,750,384]{3,2,1,0:T(8,128)(2,1)}, u32[]{:S(2)}, u32[]{:S(2)}) %all-to-all-start.3) | async-done | bytes 1152032 | tf_op jit(solution)/shard_map/all_to_all | solution.py:143
  283.6 10.8 %multiply_convert_fusion = (bf16[750,3072]{1,0:T(8,128)(2,1)}, f32[750,3072]{1,0:T(8,128)}) fusion(f32[3072]{0:T(1024)S(1)} %convert_element_type.111, bf16[768,3072]{1,0:T(8,128)(2,1)} %all-gather.9.cloned.1.call-done, f32[750,768]{1,0:T(8,128)} %copy-done, f32[768]{0:T(1024)S(1)} %convert_element_type.109, f32[768]{0:T(1024)S(1)} %convert_element_type.108, ...), kind=kOutput, calls=%fused_computation.62 | convolution fusion | flops 3555648000 | bytes 20871024 | tf_op jit(solution)/shard_map/dot_general | solution.py:168
  294.4 10.0 fusion.96
  304.4 4.8 multiply_reduce_fusion
  313.6 4.8 copy.84
  318.4 9.1 reduce.14
  327.5 4.1 reshape.286
  331.6 3.6 all-to-all-start.4
  335.3 4.5 fusion.82
  339.8 5.4 all-to-all-done.4
  345.2 4.3 reshape.287
  357.8 93.8 %while.27 = (s32[]{:T(128)}, bf16[6,1500,64]{1,2,0:T(8,128)(2,1)}, bf16[6,1500,64]{1,2,0:T(8,128)(2,1)}, bf16[6,1500,64]{1,2,0:T(8,128)(2,1)}, bf16[6,1500,64]{2...) while((s32[]{:T(128)}, bf16[6,1500,64]{1,2,0:T(8,128)(2,1)}, ...), condition=%wide.region_12.13_spmd, body=%wide.region_10.12_spmd.sunk | while | flops 1454362368 | bytes 45485876 | solution.py:220
  393.5 3.4 fusion.145
  451.6 6.8 copy.91
  458.4 10.3 %reduce.17 = bf16[1500,384]{1,0:T(8,128)(2,1)} reduce(bf16[1500,1,384]{2,1,0:T(2,128)(2,1)S(1)} %bitcast.267, bf16[]{:T(256)} %broadcast.143), dimensions={1}, to_apply=%bitcast.190.reduce_sub_computation | reduce | bytes 2304002
  468.7 3.9 reshape.292
  472.6 4.5 all-to-all-start.5
  477.1 4.1 copy.93
  481.2 9.9 reduce.16
  491.1 3.9 reshape.290
  495.0 4.4 all-to-all-start.6
  499.4 4.1 copy.95
  503.6 8.8 reduce.15
  514.9 4.5 reshape.293
  519.5 4.5 all-to-all-start.7
  524.0 10.0 bitcast_reduce_fusion
  537.0 4.5 reshape.291
  541.5 9.9 bitcast_reduce_fusion.1
  554.3 4.5 reshape.289
  558.8 9.9 bitcast_reduce_fusion.2
  572.0 8.3 fusion.72
  582.0 8.9 fusion.68
  590.9 10.8 %fusion.79 = f32[3072,768]{1,0:T(8,128)} fusion(bf16[750,3072]{1,0:T(8,128)(2,1)} %get-tuple-element.305, bf16[1,750,768]{2,1,0:T(8,128)(2,1)} %param.31), kind=kOutput, calls=%fused_computation.115 | convolution fusion | flops 3538944000 | bytes 15197184 | tf_op jit(solution)/shard_map/dot_general | solution.py:181
  604.1 9.1 fusion.75
  615.0 60.9 %reduce-scatter.5.cloned.1.call-done = f32[48,2304]{1,0:T(8,128)} async-done(((f32[768,2304]{1,0:T(8,128)}), f32[48,2304]{1,0:T(8,128)}) %reduce-scatter.5.cloned.1.call-update) | async-done | bytes 442384 | tf_op jit(solution)/shard_map/reduce_scatter | solution.py:270
  675.9 115.0 %reduce-scatter.9.cloned.1.call-done = f32[48,3072]{1,0:T(8,128)} async-done(((f32[768,3072]{1,0:T(8,128)}), f32[48,3072]{1,0:T(8,128)}) %reduce-scatter.9.cloned.1.call-update) | async-done | bytes 589840 | tf_op jit(solution)/shard_map/reduce_scatter | solution.py:204
  790.9 115.0 %reduce-scatter.11.cloned.1.call-done = f32[192,768]{1,0:T(8,128)} async-done(((f32[3072,768]{1,0:T(8,128)}), f32[192,768]{1,0:T(8,128)}) %reduce-scatter.11.cloned.1.call-update) | async-done | bytes 589840 | tf_op jit(solution)/shard_map/reduce_scatter | solution.py:205
  906.0 7.9 fusion.63
  914.0 60.9 %all-reduce.16 = (f32[768]{0:T(1024)S(1)}, f32[768]{0:T(1024)}, f32[1536]{0:T(1024)S(1)}, f32[768]{0:T(1024)}, f32[768]{0:T(1024)}, /*index=5*/f32[768]{0:T(1024)}, f32[3072]{0:T(1024)S(1)}, f32[768]{0:T(1024)}) all-reduce(f32[768]{0:T(1024)S(1)} %get-tuple-element.222, ...), channel_id=2, replica_groups=mesh['dp'=16,'seq'=2] {'dp'}, use_global_device_ids=true, to_apply=%region_17.18.clone | all-reduce | flops 9216 | bytes 73728
  980.9 3.8 copy.97
  984.9 5.5 all-reduce.17
  (275 shorter events, 221.0 us)
Async XLA Ops:
  7.2 77.7 %copy-start.4 = (bf16[1,750,768]{2,1,0:T(8,128)(2,1)S(1)}, bf16[1,750,768]{2,1,0:T(8,128)(2,1)}, u32[]{:S(2)}) copy-start(bf16[1,750,768]{2,1,0:T(8,128)(2,1)} %param.18) | copy-start | bytes 3456004
  7.2 78.3 %all-gather.5.cloned.1.call-start = ((), (), s32[]{:S(2)}) async-start(), calls=%async_computation.12 | async-start | bytes 3760128 | tf_op jit(solution)/shard_map/all_gather | solution.py:109
  7.9 270.9 %all-gather.7.cloned.1.call-start = ((), (), s32[]{:S(2)}) async-start(), calls=%async_computation.13 | async-start | bytes 1253376 | tf_op jit(solution)/shard_map/all_gather | solution.py:110
  8.7 274.9 %all-gather.9.cloned.1.call-start = ((), (), s32[]{:S(2)}) async-start(), calls=%async_computation.14 | async-start | bytes 5013504 | tf_op jit(solution)/shard_map/all_gather | solution.py:156
  83.4 7.2 copy-start.20
  83.4 7.2 copy-start.25
  84.9 5.7 copy-start.16
  85.4 5.2 copy-start.22
  90.6 3.2 copy-start.9
  112.4 4.6 copy-start.13
  112.4 22.6 %all-to-all-start = ((bf16[2,2,144000]{2,1,0:T(2,128)(2,1)}), bf16[2,2,144000]{2,1,0:T(2,128)(2,1)}, u32[]{:S(2)}, u32[]{:S(2)}) async-start(bf16[2,2,144000]{2,1,0:T(2,128)(2,1)} %reshape.280), calls=%async_computation | async-start | bytes 2304000 | tf_op jit(solution)/shard_map/all_to_all | solution.py:129
  135.0 24.5 %all-to-all-start.2 = ((bf16[2,2,144000]{2,1,0:T(2,128)(2,1)}), bf16[2,2,144000]{2,1,0:T(2,128)(2,1)}, u32[]{:S(2)}, u32[]{:S(2)}) async-start(bf16[2,2,144000]{2,1,0:T(2,128)(2,1)} %reshape.284), calls=%async_computation.2 | async-start | bytes 2304000 | tf_op jit(solution)/shard_map/all_to_all | solution.py:133
  159.5 35.0 %all-to-all-start.1 = ((bf16[2,2,144000]{2,1,0:T(2,128)(2,1)}), bf16[2,2,144000]{2,1,0:T(2,128)(2,1)}, u32[]{:S(2)}, u32[]{:S(2)}) async-start(bf16[2,2,144000]{2,1,0:T(2,128)(2,1)} %reshape.282), calls=%async_computation.1 | async-start | bytes 2304000 | tf_op jit(solution)/shard_map/all_to_all | solution.py:130
  164.0 130.4 %all-gather.11.cloned.1.call-start = ((), (), s32[]{:S(2)}) async-start(), calls=%async_computation.15 | async-start | bytes 5013504 | tf_op jit(solution)/shard_map/all_gather | solution.py:157
  260.6 15.5 %all-to-all-start.3 = ((bf16[2,1,750,384]{3,2,1,0:T(8,128)(2,1)}), bf16[2,1,750,384]{3,2,1,0:T(8,128)(2,1)}, u32[]{:S(2)}, u32[]{:S(2)}) async-start(bf16[2,1,750,384]{3,2,1,0:T(8,128)(2,1)} %copy.82), calls=%async_computation.3 | async-start | bytes 2310144 | tf_op jit(solution)/shard_map/all_to_all | solution.py:143
  281.7 1.4 copy-start
  283.5 10.9 %copy-start.14 = (bf16[1,750,768]{2,1,0:T(8,128)(2,1)S(1)}, bf16[1,750,768]{2,1,0:T(8,128)(2,1)}, u32[]{:S(2)}) copy-start(bf16[1,750,768]{2,1,0:T(8,128)(2,1)} %param.31) | copy-start | bytes 3456004
  294.4 10.0 copy-start.1
  294.4 10.0 copy-start.30
  304.4 4.8 copy-start.12
  309.2 3.2 copy-start.31
  311.0 1.4 copy-start.7
  331.6 13.5 %all-to-all-start.4 = ((bf16[2,2,144000]{2,1,0:T(2,128)(2,1)}), bf16[2,2,144000]{2,1,0:T(2,128)(2,1)S(1)}, u32[]{:S(2)}, u32[]{:S(2)}) async-start(bf16[2,2,144000]{2,1,0:T(2,128)(2,1)} %reshape.286), calls=%async_computation.4 | async-start | bytes 2304000 | tf_op jit(solution)/shard_map/all_to_all | solution.py:217
  335.2 279.8 %reduce-scatter.7.cloned.1.call-start = ((), (), s32[]{:S(2)}) async-start(), calls=%async_computation.17 | async-start | bytes 2506752 | tf_op jit(solution)/shard_map/reduce_scatter | solution.py:271
  468.7 8.4 copy-start.10
  472.6 22.4 %all-to-all-start.5 = ((bf16[2,2,144000]{2,1,0:T(2,128)(2,1)}), bf16[2,2,144000]{2,1,0:T(2,128)(2,1)}, u32[]{:S(2)}, u32[]{:S(2)}) async-start(bf16[2,2,144000]{2,1,0:T(2,128)(2,1)} %reshape.292), calls=%async_computation.5 | async-start | bytes 2304000 | tf_op jit(solution)/shard_map/all_to_all | solution.py:232
  491.1 8.3 copy-start.11
  495.0 24.5 %all-to-all-start.6 = ((bf16[2,2,144000]{2,1,0:T(2,128)(2,1)}), bf16[2,2,144000]{2,1,0:T(2,128)(2,1)}, u32[]{:S(2)}, u32[]{:S(2)}) async-start(bf16[2,2,144000]{2,1,0:T(2,128)(2,1)} %reshape.290), calls=%async_computation.6 | async-start | bytes 2304000 | tf_op jit(solution)/shard_map/all_to_all | solution.py:235
  519.5 34.9 %all-to-all-start.7 = ((bf16[2,2,144000]{2,1,0:T(2,128)(2,1)}), bf16[2,2,144000]{2,1,0:T(2,128)(2,1)}, u32[]{:S(2)}, u32[]{:S(2)}) async-start(bf16[2,2,144000]{2,1,0:T(2,128)(2,1)} %reshape.288), calls=%async_computation.7 | async-start | bytes 2304000 | tf_op jit(solution)/shard_map/all_to_all | solution.py:238
  524.0 151.9 %reduce-scatter.5.cloned.1.call-start = ((), (), s32[]{:S(2)}) async-start(), calls=%async_computation.16 | async-start | bytes 7520256 | tf_op jit(solution)/shard_map/reduce_scatter | solution.py:270
  568.7 3.3 copy-start.5
  568.7 3.3 copy-start.17
  568.7 3.3 copy-start.21
  568.7 3.3 copy-start.23
  568.7 3.3 copy-start.26
  570.3 10.0 copy-start.3
  580.3 1.7 copy-start.2
  580.3 210.6 %reduce-scatter.9.cloned.1.call-start = ((), (), s32[]{:S(2)}) async-start(), calls=%async_computation.18 | async-start | bytes 10027008 | tf_op jit(solution)/shard_map/reduce_scatter | solution.py:204
  590.9 315.0 %reduce-scatter.11.cloned.1.call-start = ((), (), s32[]{:S(2)}) async-start(), calls=%async_computation.19 | async-start | bytes 10027008 | tf_op jit(solution)/shard_map/reduce_scatter | solution.py:205
  601.8 2.3 copy-start.29
  601.8 388.6 %all-reduce.22.cloned.1.call-start = ((), (), s32[]{:S(2)}) async-start(), calls=%async_computation.20 | async-start | bytes 3538944 | tf_op jit(solution)/shard_map/psum | solution.py:265
  613.2 292.8 %copy-start.6 = (bf16[1,750,768]{2,1,0:T(8,128)(2,1)S(1)}, bf16[1,750,768]{2,1,0:T(8,128)(2,1)}, u32[]{:S(2)}) copy-start(bf16[1,750,768]{2,1,0:T(8,128)(2,1)} %param.18) | copy-start | bytes 3456004
  906.0 8.0 copy-start.18
  906.0 8.0 copy-start.19
  906.0 8.0 copy-start.24
  906.0 8.0 copy-start.27
  906.0 8.0 copy-start.28
  906.0 72.7 %copy-start.8 = (f32[750,768]{1,0:T(8,128)S(1)}, f32[750,768]{1,0:T(8,128)}, u32[]{:S(2)}) copy-start(f32[750,768]{1,0:T(8,128)} %copy-done.7) | copy-start | bytes 6912004
  990.4 5.4 copy-start.15
Sparse Core Ops, SparseCore 0:
  10.3 50.1 all-gather.4
  62.8 36.8 all-gather.6
  101.9 51.9 all-gather.8
  166.8 50.9 all-gather.10
  339.9 63.1 reduce-scatter.6
  580.5 95.3 reduce-scatter.4
  680.0 110.9 reduce-scatter.8
  795.0 110.8 reduce-scatter.10
  908.4 55.5 all-reduce.21
